TPU v7x, 256 devices: a whole 4x4x8 slice. The times are simulated.
256 devices in a mesh: env: 4 (over x_lo, core), tm: 64 (over x_hi, z, y).
Axes of the slice: x: 4 (x_hi: 2, x_lo: 2; x = x_hi * 2 + x_lo), y: 4, z: 8, core: 2. Of those that a mesh axis runs over, the one named last changes fastest.
Arguments:
- hidden: bfloat16 [4, 64, 256, 1024], P('env', 'tm'), may hold values from -6 to 6
- done_step: int32 [4, 64], P('env', 'tm'), may hold values from 0 to 255
- alive: int32 [4, 64, 256], P('env', None, 'tm'), may hold values 0 or 1
- targets: float32 [4, 64, 256], P('env', None, 'tm'), may hold values from -6 to 6
- gain_t: float32 [1024], replicated, may hold values from 0.25 to 1.75
- w_qkv_t: bfloat16 [1024, 3072], replicated, may hold values from -5 to 5
- w_out_t: bfloat16 [1024, 1024], replicated, may hold values from -0.1875 to 0.1875
- gain_a: float32 [1024], replicated, may hold values from 0.25 to 1.75
- w_qkv_a: bfloat16 [1024, 3072], P('tm'), may hold values from -5 to 5
- w_out_a: bfloat16 [1024, 1024], P('tm'), may hold values from -0.1875 to 0.1875
- w_value: float32 [1024], replicated, may hold values from -0.1875 to 0.1875
Outputs:
- values: float32 [4, 64, 256], P('env', None, 'tm')
- input_grad: bfloat16 [4, 64, 256, 1024], P('env', 'tm')
- qkv_grad: float32 [1024, 3072], P('tm')
- out_grad: float32 [1024, 1024], P('tm')
Inputs may be any that keep to these rules, and one draw needn't show every extreme that they name: `done_step`: the last step of an agent's first episode in the window; later steps form a new episode.
All inputs are finite; a program needn't handle non-finite values. No bound on the sum of `alive` on one device may be relied on, other than what follows from the above.
Results may differ from a plain program's by a relative error of at most 0.02.
Values may be sent and summed in bfloat16 or wider, within the bound.
A program may use at most 128 MiB of HBM per device.

v0:
```python
import math
import jax
import jax.numpy as jnp
from jax import lax
from jax.sharding import PartitionSpec as P

HEADS = 8
HI = lax.Precision.HIGHEST


def norm_scale(rows, gain):
    return rows * lax.rsqrt(jnp.mean(rows * rows, axis=-1, keepdims=True) + 1e-06) * gain


def attend(qkv, allowed, head_count):
    width = qkv.shape[-1] // 3
    size = width // head_count
    shape = qkv.shape[:-1] + (head_count, size)
    queries = qkv[..., :width].reshape(shape)
    key_rows = qkv[..., width : 2 * width].reshape(shape)
    value_rows = qkv[..., 2 * width :].reshape(shape)
    scores = jnp.einsum("qhe,khe->hqk", queries, key_rows, preferred_element_type=jnp.float32)
    scores = jnp.where(allowed[None], scores / math.sqrt(size), -1e30)
    row_max = jnp.max(scores, axis=-1, keepdims=True)
    weights = jnp.exp(scores - row_max)
    probs = (weights / jnp.sum(weights, axis=-1, keepdims=True)).astype(jnp.bfloat16)
    mixed = jnp.einsum("hqk,khe->qhe", probs, value_rows, preferred_element_type=jnp.float32)
    return mixed.reshape(qkv.shape[:-1] + (width,))


def temporal_block(rows, done, gain, w_qkv, w_out, head_count):
    length, width = rows.shape
    rows_f = rows.astype(jnp.float32)
    normed = norm_scale(rows_f, gain).astype(jnp.bfloat16)
    qkv = jnp.dot(normed, w_qkv, preferred_element_type=jnp.float32).astype(jnp.bfloat16)
    positions = jnp.arange(length, dtype=jnp.int32)
    later = positions > done
    allowed = (positions[:, None] >= positions[None, :]) & (later[:, None] == later[None, :])
    mixed = attend(qkv, allowed, head_count).astype(jnp.bfloat16)
    added = jnp.dot(mixed, w_out, preferred_element_type=jnp.float32)
    return (rows_f + added).astype(jnp.bfloat16)


def left_product(left, right):
    return lax.dot_general(
        left, right, (((0,), (0,)), ((), ())), preferred_element_type=jnp.float32
    )


def agent_step(lifted, alive_rows, target_rows, gain, w_qk, z, w_value, head_count):
    agent_count, step_count, width = lifted.shape
    size = width // head_count
    lifted_f = lifted.astype(jnp.float32)
    normed_f, norm_pull = jax.vjp(lambda rows: norm_scale(rows, gain), lifted_f)
    normed = normed_f.astype(jnp.bfloat16).reshape(-1, width)
    qk = jnp.dot(normed, w_qk, preferred_element_type=jnp.float32).astype(jnp.bfloat16)
    qk = qk.reshape(agent_count, step_count, 2, head_count, size)
    q, k = (qk[:, :, 0], qk[:, :, 1])
    s = jnp.dot(normed.astype(jnp.float32), z, precision=HI)
    s = s.reshape(agent_count, step_count, head_count).transpose(1, 2, 0)
    living = alive_rows.T == 1
    allowed = living[:, None, :] | jnp.eye(agent_count, dtype=bool)[None]
    scores = jnp.einsum("qbhe,kbhe->bhqk", q, k, preferred_element_type=jnp.float32)
    scores = jnp.where(allowed[:, None], scores / math.sqrt(size), -1e30)
    weights = jnp.exp(scores - jnp.max(scores, axis=-1, keepdims=True))
    probs = weights / jnp.sum(weights, axis=-1, keepdims=True)
    pv = jnp.sum(probs * s[:, :, None, :], axis=-1)
    predicted = jnp.sum(lifted_f * w_value, axis=-1) + jnp.sum(pv, axis=1).T
    err = 32.0 * alive_rows.astype(jnp.float32) * (predicted - target_rows)
    weighted = probs * err.T[:, None, :, None]
    t = jnp.sum(weighted, axis=2)
    ds = weighted * (s[:, :, None, :] - pv[..., None]) * (1.0 / math.sqrt(size))
    ds = ds.astype(jnp.bfloat16)
    dq = jnp.einsum("bhqk,kbhe->qbhe", ds, k, preferred_element_type=jnp.float32)
    dk = jnp.einsum("bhqk,qbhe->kbhe", ds, q, preferred_element_type=jnp.float32)
    dqk = jnp.stack([dq, dk], axis=2).astype(jnp.bfloat16).reshape(-1, 2 * width)
    t = t.transpose(2, 0, 1).reshape(-1, head_count)
    grad_normed = jnp.dot(dqk, w_qk.T, preferred_element_type=jnp.float32)
    grad_normed = grad_normed + jnp.dot(t, z.T, precision=HI)
    grad_top = err[..., None] * w_value
    grad_lifted = grad_top + norm_pull(grad_normed.reshape(agent_count, step_count, width))[0]
    return (predicted, grad_lifted.astype(jnp.bfloat16), normed, dqk, t)


def per_device(
    hidden, done_step, alive, targets, gain_t, w_qkv_t, w_out_t, gain_a, w_qkv_a, w_out_a, w_value
):
    width = hidden.shape[-1]
    size = width // HEADS
    local_rows = hidden[0, 0]
    done = done_step[0, 0]
    v = lax.all_gather(
        jnp.sum(w_out_a.astype(jnp.float32) * w_value, axis=1), "tm", axis=0, tiled=True
    )
    w_v = w_qkv_a[:, 2 * width :].astype(jnp.float32)
    z = jnp.sum((w_v * v).reshape(-1, HEADS, size), axis=-1)
    z = lax.all_gather(z, "tm", axis=0, tiled=True)
    w_qk = lax.all_gather(w_qkv_a[:, : 2 * width], "tm", axis=0, tiled=True)
    first, pull = jax.vjp(
        lambda rows: temporal_block(rows, done, gain_t, w_qkv_t, w_out_t, HEADS), local_rows
    )
    lifted = lax.all_to_all(first[None], "tm", split_axis=1, concat_axis=0, tiled=True)
    predicted, grad_lifted, normed, dqk, t = agent_step(
        lifted, alive[0], targets[0], gain_a, w_qk, z, w_value, HEADS
    )
    returned = lax.all_to_all(grad_lifted, "tm", split_axis=0, concat_axis=1, tiled=True)
    terms = left_product(normed, dqk).astype(jnp.bfloat16)
    u_terms = lax.dot_general(normed.astype(jnp.float32), t, (((0,), (0,)), ((), ())), precision=HI)
    summed = lax.psum_scatter(terms, "tm", scatter_dimension=0, tiled=True)
    qk_grad = lax.psum(summed, "env").astype(jnp.float32)
    u_mine = lax.psum(u_terms, ("env", "tm"))
    u_mine = lax.dynamic_slice_in_dim(u_mine, lax.axis_index("tm") * w_v.shape[0], w_v.shape[0], 0)
    u_wide = jnp.repeat(u_mine, size, axis=1)
    v_grad = u_wide * v
    mixed_err = lax.psum(jnp.sum(u_wide * w_v, axis=0), "tm")
    mixed_err = lax.dynamic_slice_in_dim(
        mixed_err, lax.axis_index("tm") * w_out_a.shape[0], w_out_a.shape[0], 0
    )
    out_grad = mixed_err[:, None] * w_value
    qkv_grad = jnp.concatenate([qk_grad, v_grad], axis=1)
    input_grad = pull(returned[0])[0]
    return (predicted[None], input_grad[None, None], qkv_grad, out_grad)


def solution(mesh):
    in_specs = (
        P("env", "tm", None, None),
        P("env", "tm"),
        P("env", None, "tm"),
        P("env", None, "tm"),
        P(),
        P(),
        P(),
        P(),
        P("tm", None),
        P("tm", None),
        P(),
    )
    out_specs = (P("env", None, "tm"), P("env", "tm", None, None), P("tm", None), P("tm", None))
    return jax.shard_map(
        per_device, mesh=mesh, in_specs=in_specs, out_specs=out_specs, check_vma=False
    )
```

profile of v0, /device:TPU:1, one launch (start us, length us, event | category | flops | bytes accessed | tf_op | source)
XLA Modules:
  0.0 856.8 jit_solution(7488116643575696525)
XLA Ops:
  7.2 1.6 slice.24
  9.5 1.2 fusion.49
  10.7 0.5 copy-done.25
  11.3 4.9 convolution_convert_fusion
  16.1 1.1 slice_bitcast_fusion
  17.2 1.4 copy.98
  18.7 2.2 copy.97
  21.0 1.6 fusion.114
  23.3 0.7 copy-done.1
  24.0 1.0 copy-done.3
  25.4 0.7 fusion.37
  26.1 0.8 copy.135
  27.0 0.5 broadcast.202
  27.5 4.5 reduce.4
  32.0 2.2 reshape.279
  34.2 15.1 %all-to-all-start = ((bf16[64,2,2048]{2,1,0:T(2,128)(2,1)}), bf16[64,2,2048]{2,1,0:T(2,128)(2,1)S(1)}, u32[]{:S(2)}, u32[]{:S(2)}) async-start(bf16[64,2,2048]{2,1,0:T(2,128)(2,1)} %reshape.279), calls=%async_computation | async-start | bytes 1048576 | tf_op jit(solution)/shard_map/all_to_all | solution.py:102
  49.4 0.6 dynamic-slice
  51.0 156.9 %all-reduce.3 = f32[1024]{0:T(1024)S(1)} all-reduce(f32[1024]{0:T(1024)S(1)} %dynamic-update-slice), channel_id=1, replica_groups=mesh['env'=4,'tm'=64] {'tm'}, use_global_device_ids=true, to_apply=%add.3 | all-reduce | flops 1024 | bytes 8192
  207.9 0.8 fusion.93
  208.9 148.0 %all-gather = f32[64,16,8]{1,2,0:T(8,128)S(1)} all-gather(f32[1,16,8]{1,2,0:T(8,128)S(1)} %bitcast.169), channel_id=1, replica_groups=mesh['env'=4,'tm'=64] {'tm'}, dimensions={0}, use_global_device_ids=true | all-gather | bytes 33280 | tf_op jit(solution)/shard_map/all_gather | solution.py:97
  357.2 0.7 broadcast_or_fusion
  357.9 1.8 reshape.280
  359.7 1.6 fusion.39
  361.5 0.7 copy.75
  362.2 1.3 reshape.268
  363.5 1.5 multiply_convert_fusion
  365.0 0.8 copy-done.6
  365.8 1.3 convolution_bitcast_fusion.3
  367.1 3.5 fusion.16
  370.9 1.0 fusion.113
  371.9 3.5 multiply_reduce_fusion.2
  375.4 1.3 fusion.95
  376.7 3.3 convolution_bitcast_fusion
  380.0 3.4 convolution_bitcast_fusion.1
  383.5 1.3 maximum_convert_fusion
  384.8 1.7 copy.78
  386.4 2.3 convert_element_type.173
  388.7 4.6 convolution_convert_fusion.1
  393.5 0.5 copy-done.22
  394.1 1.6 multiply_reduce_fusion
  395.8 3.8 fusion.115
  399.6 2.1 fusion.40
  401.8 2.6 reshape.260
  404.4 2.8 fusion.47
  407.2 4.9 all-to-all-start.1
  412.1 1.5 convolution_bitcast_fusion.2
  413.6 132.2 %psum.22 = f32[1024,8]{0,1:T(8,128)S(1)} all-reduce(f32[1024,8]{0,1:T(8,128)S(1)} %convolution_bitcast_fusion.2), channel_id=1, replica_groups=mesh['env'=4,'tm'=64] {'env','tm'}, use_global_device_ids=true, to_apply=%region_19.20 | all-reduce | flops 8192 | bytes 65536 | tf_op jit(solution)/shard_map/psum | solution.py:111
  546.0 0.8 fusion.94
  546.8 156.0 %psum.23 = f32[1024]{0:T(1024)S(1)} all-reduce(f32[1024]{0:T(1024)S(1)} %get-tuple-element.19), channel_id=1, replica_groups=mesh['env'=4,'tm'=64] {'tm'}, use_global_device_ids=true, to_apply=%region_21.22 | all-reduce | flops 1024 | bytes 8192 | tf_op jit(solution)/shard_map/psum | solution.py:115
  702.9 0.7 broadcast_multiply_fusion
  703.6 0.9 squeeze.21
  704.6 2.6 convolution_convert_fusion.5
  707.2 1.2 copy.94
  708.5 2.3 fusion.6
  710.9 1.0 convert_reduce_fusion
  712.6 1.2 fusion.25
  713.8 1.2 fusion.24
  715.2 0.7 slice-done.1
  716.0 2.9 fusion.52
  718.9 45.1 %reduce-scatter.2.cloned.1.call-done = bf16[16,2048]{1,0:T(8,128)(2,1)} async-done(((bf16[1024,2048]{1,0:T(8,128)(2,1)}), bf16[16,2048]{1,0:T(8,128)(2,1)}) %reduce-scatter.2.cloned.1.call-update) | async-done | bytes 65552 | tf_op jit(solution)/shard_map/reduce_scatter | solution.py:109
  764.1 2.3 fusion.67
  766.4 82.4 %all-reduce.6.cloned.1.call-done = bf16[16,2048]{1,0:T(8,128)(2,1)} async-done(((bf16[16,2048]{1,0:T(8,128)(2,1)}), bf16[16,2048]{1,0:T(8,128)(2,1)}) %all-reduce.6.cloned.1.call-update) | async-done | bytes 65552 | tf_op jit(solution)/shard_map/psum | solution.py:110
  848.8 0.8 convert_element_type.192
  849.6 0.7 pad_maximum_fusion
  (107 shorter events, 4.4 us)
Async XLA Ops:
  7.2 18.2 %copy-start = (bf16[1024,1024]{1,0:T(8,128)(2,1)S(1)}, bf16[1024,1024]{1,0:T(8,128)(2,1)}, u32[]{:S(2)}) copy-start(bf16[1024,1024]{1,0:T(8,128)(2,1)} %param.17) | copy-start | bytes 6291460
  7.2 359.9 %all-gather.3.cloned.1.call-start = ((), (), s32[]{:S(2)}) async-start(), calls=%async_computation.3 | async-start | bytes 4259840 | tf_op jit(solution)/shard_map/all_gather | solution.py:98
  10.7 0.5 copy-start.25
  11.3 4.9 copy-start.28
  17.2 6.8 copy-start.9
  18.7 3.9 copy-start.11
  22.6 1.4 copy-start.1
  22.9 2.4 copy-start.16
  22.9 2.4 copy-start.7
  24.0 1.0 copy-start.3
  26.9 22.4 %copy-start.31 = (u32[256]{0:T(256)S(1)}, u32[256]{0:T(256)}, u32[]{:S(2)}) copy-start(u32[256]{0:T(256)} %constant.61) | copy-start | bytes 3076
  26.9 23.7 %copy-start.18 = (f32[1024]{0:T(1024)S(1)}, f32[1024]{0:T(1024)}, u32[]{:S(2)}) copy-start(f32[1024]{0:T(1024)} %param.21) | copy-start | bytes 12292
  27.0 23.7 %copy-start.21 = (bf16[16,1024]{1,0:T(8,128)(2,1)S(1)}, bf16[16,1024]{1,0:T(8,128)(2,1)}, u32[]{:S(2)}) copy-start(bf16[16,1024]{1,0:T(8,128)(2,1)} %param.20) | copy-start | bytes 98308
  32.0 325.1 %copy-start.27 = (s32[1,64,4]{1,2,0:T(4,128)S(1)}, s32[1,64,4]{1,2,0:T(4,128)}, u32[]{:S(2)}) copy-start(s32[1,64,4]{1,2,0:T(4,128)} %param.13) | copy-start | bytes 3076
  34.2 323.7 %all-to-all-start = ((bf16[64,2,2048]{2,1,0:T(2,128)(2,1)}), bf16[64,2,2048]{2,1,0:T(2,128)(2,1)S(1)}, u32[]{:S(2)}, u32[]{:S(2)}) async-start(bf16[64,2,2048]{2,1,0:T(2,128)(2,1)} %reshape.279), calls=%async_computation | async-start | bytes 1048576 | tf_op jit(solution)/shard_map/all_to_all | solution.py:102
  49.3 714.7 %reduce-scatter.2.cloned.1.call-start = ((), (), s32[]{:S(2)}) async-start(), calls=%async_computation.4 | async-start | bytes 4259840 | tf_op jit(solution)/shard_map/reduce_scatter | solution.py:109
  207.9 149.2 %copy-start.19 = (f32[1024]{0:T(1024)}, f32[1024]{0:T(1024)S(1)}, u32[]{:S(2)}) copy-start(f32[1024]{0:T(1024)S(1)} %all-reduce.3) | copy-start | bytes 12292
  357.9 5.6 copy-start.15
  361.3 9.4 %copy-start.23 = (f32[256]{0:T(256)}, f32[256]{0:T(256)S(1)}, u32[]{:S(2)}) copy-start(f32[256]{0:T(256)S(1)} %get-tuple-element.24) | copy-start | bytes 3076
  365.0 0.8 copy-start.6
  384.8 4.0 copy-start.24
  393.3 0.7 copy-start.22
  401.7 2.7 copy-start.5
  404.4 7.7 copy-start.17
  404.4 141.6 %copy-start.20 = (f32[1024]{0:T(1024)S(1)}, f32[1024]{0:T(1024)}, u32[]{:S(2)}) copy-start(f32[1024]{0:T(1024)} %copy-done.19) | copy-start | bytes 12292
  407.2 296.4 %all-to-all-start.1 = ((bf16[64,4,1024]{2,1,0:T(4,128)(2,1)}), bf16[64,4,1024]{2,1,0:T(4,128)(2,1)S(1)}, u32[]{:S(2)}, u32[]{:S(2)}) async-start(bf16[64,4,1024]{2,1,0:T(4,128)(2,1)} %fusion.47), calls=%async_computation.1 | async-start | bytes 1048576 | tf_op jit(solution)/shard_map/all_to_all | solution.py:106
  412.0 436.7 %all-reduce.6.cloned.1.call-start = ((), (), s32[]{:S(2)}) async-start(), calls=%async_computation.5 | async-start | bytes 131072 | tf_op jit(solution)/shard_map/psum | solution.py:110
  704.6 3.9 copy-start.10
  708.5 2.4 copy-start.2
  710.8 1.2 copy-start.4
  710.8 1.7 copy-start.12
  712.5 1.2 copy-start.13
  712.5 2.4 slice-start
  713.8 1.5 copy-start.8
  713.8 2.2 slice-start.1
  713.8 2.2 copy-start.30
  716.0 2.9 copy-start.26
  716.0 48.0 %copy-start.14 = (bf16[256,1024]{1,0:T(8,128)(2,1)S(1)}, bf16[256,1024]{1,0:T(8,128)(2,1)}, u32[]{:S(2)}) copy-start(bf16[256,1024]{1,0:T(8,128)(2,1)} %squeeze.21) | copy-start | bytes 1572868
  716.0 48.0 %copy-start.29 = (f32[256]{0:T(256)S(1)}, f32[256]{0:T(256)}, u32[]{:S(2)}) copy-start(f32[256]{0:T(256)} %copy-done.28) | copy-start | bytes 3076
Sparse Core Ops, SparseCore 0:
  12.1 128.8 all-gather.2
  393.4 370.5 reduce-scatter.1
  766.8 81.8 all-reduce.5
where the time goes:
time: 858 us; the launch traced here: 857 us
  blocking collectives  593 us (69%)
  waiting for transfers between devices  128 us (15%)
  matrix products  45.3 us (5%)
  local copies, waits for them, and re-layouts  30.5 us (4%)
  other arithmetic  24.6 us (3%)
  starting transfers between devices  20.1 us (2%)
  between operations  15.7 us (2%)
    unnamed x1, blocking collectives  157 us
    psum x1, blocking collectives, per_device(): mixed_err = lax.psum(jnp.sum(u_wide * w_v, axis=0), 'tm')  156 us
    all_gather x1, blocking collectives, per_device(): z = lax.all_gather(z, 'tm', axis=0, tiled=True)  148 us
    psum x1, blocking collectives, per_device(): u_mine = lax.psum(u_terms, ('env', 'tm'))  132 us
    psum x1, waiting for transfers between devices, per_device(): qk_grad = lax.psum(summed, 'env').astype(jnp.float32)  82.4 us
    reduce_scatter x1, waiting for transfers between devices, per_device(): summed = lax.psum_scatter(terms, 'tm', scatter_dimension=0, tiled=True)  45.1 us
  transfers between devices with their start and end apart: 5, of which 2 were waited for; matrix products, arithmetic and copies ran while one was open for 8% of the time, Pallas kernels for 0%

commit v1 on v0

--- a/solution.py
+++ b/solution.py
@@ -94,7 +94,7 @@
     )
     w_v = w_qkv_a[:, 2 * width :].astype(jnp.float32)
     z = jnp.sum((w_v * v).reshape(-1, HEADS, size), axis=-1)
-    z = lax.all_gather(z, "tm", axis=0, tiled=True)
+    z = jnp.concatenate(lax.all_to_all(jnp.stack([z] * lax.axis_size("tm")), "tm", 0, 0), axis=0)
     w_qk = lax.all_gather(w_qkv_a[:, : 2 * width], "tm", axis=0, tiled=True)
     first, pull = jax.vjp(
         lambda rows: temporal_block(rows, done, gain_t, w_qkv_t, w_out_t, HEADS), local_rows

time: 858 us -> 711 us (0.83)
  blocking collectives: 593 us -> 423 us
  local copies, waits for them, and re-layouts: 30.5 us -> 40.9 us
    all_gather x1 -> x0, blocking collectives: 148 us -> none  [per_device(): z = lax.all_gather(z, 'tm', axis=0, tiled=True)]
    psum x1, blocking collectives: 132 us -> 107 us  [per_device(): u_mine = lax.psum(u_terms, ('env', 'tm'))]
    all_to_all x1, waiting for transfers between devices: 0.01 us -> 9.59 us  [per_device(): lax.all_to_all(first[None], 'tm', split_axis=1, concat_axis=0, tiled=True)]
  transfers between devices with their start and end apart: 5 -> 6, of which waited for: 2 -> 3; matrix products, arithmetic and copies ran while one was open for 8% -> 12% of each run, Pallas kernels for 0% -> 0%
where the time goes in v1:
time: 711 us; the launch traced here: 709 us
  blocking collectives  423 us (59%)
  waiting for transfers between devices  131 us (18%)
  matrix products  44.7 us (6%)
  local copies, waits for them, and re-layouts  40.9 us (6%)
  other arithmetic  30.2 us (4%)
  starting transfers between devices  23.3 us (3%)
  between operations  15.7 us (2%)
    unnamed x1, blocking collectives  161 us
    psum x1, blocking collectives, per_device(): mixed_err = lax.psum(jnp.sum(u_wide * w_v, axis=0), 'tm')  156 us
    psum x1, blocking collectives, per_device(): u_mine = lax.psum(u_terms, ('env', 'tm'))  107 us
    psum x1, waiting for transfers between devices, per_device(): qk_grad = lax.psum(summed, 'env').astype(jnp.float32)  82.8 us
    reduce_scatter x1, waiting for transfers between devices, per_device(): summed = lax.psum_scatter(terms, 'tm', scatter_dimension=0, tiled=True)  38.9 us
    unnamed x74, local copies, waits for them, and re-layouts  14.4 us
  transfers between devices with their start and end apart: 6, of which 3 were waited for; matrix products, arithmetic and copies ran while one was open for 12% of the time, Pallas kernels for 0%

profile of v1, /device:TPU:1, one launch (start us, length us, event | category | flops | bytes accessed | tf_op | source)
XLA Modules:
  0.0 709.4 jit_solution(1014976466130391429)
XLA Ops:
  7.2 1.6 slice.24
  8.9 1.3 dynamic-slice
  10.8 0.9 multiply_reduce_fusion.3
  11.9 160.8 %all-reduce.3 = f32[1024]{0:T(1024)S(1)} all-reduce(f32[1024]{0:T(1024)S(1)} %dynamic-update-slice), channel_id=1, replica_groups=mesh['env'=4,'tm'=64] {'tm'}, use_global_device_ids=true, to_apply=%add.3 | all-reduce | flops 1024 | bytes 8192
  173.3 0.8 fusion.90
  174.3 0.8 reshape.296
  175.1 4.6 all-to-all-start.1
  180.3 1.2 fusion.49
  181.6 4.9 convolution_convert_fusion
  186.5 1.1 slice_bitcast_fusion
  187.8 1.4 copy.97
  192.1 0.7 fusion.37
  192.8 1.8 copy.135
  195.1 5.6 reduce.4
  200.7 2.2 reshape.294
  202.9 12.6 %all-to-all-start = ((bf16[64,2,2048]{2,1,0:T(2,128)(2,1)}), bf16[64,2,2048]{2,1,0:T(2,128)(2,1)}, u32[]{:S(2)}, u32[]{:S(2)}) async-start(bf16[64,2,2048]{2,1,0:T(2,128)(2,1)} %reshape.294), calls=%async_computation | async-start | bytes 1048576 | tf_op jit(solution)/shard_map/all_to_all | solution.py:102
  215.8 0.7 broadcast_or_fusion
  217.0 0.7 reduce.5
  217.7 0.8 reshape.297
  218.6 1.0 copy.73
  219.7 9.6 %all-to-all-done = bf16[64,2,2048]{2,1,0:T(2,128)(2,1)} async-done(((bf16[64,2,2048]{2,1,0:T(2,128)(2,1)}), bf16[64,2,2048]{2,1,0:T(2,128)(2,1)}, u32[]{:S(2)}, u32[]{:S(2)}) %all-to-all-start) | async-done | bytes 524320 | tf_op jit(solution)/shard_map/all_to_all | solution.py:102
  229.3 4.4 reshape.295
  233.8 2.9 fusion.39
  236.6 0.8 reduce_sum.167
  238.1 1.3 multiply_add_fusion
  239.4 2.0 fusion.41
  241.4 2.1 convert_element_type.178
  243.5 1.8 convolution_bitcast_fusion.3
  245.3 3.7 fusion.16
  249.2 1.2 fusion.110
  250.4 3.0 multiply_reduce_fusion.2
  254.0 3.2 convolution_bitcast_fusion
  257.2 3.5 convolution_bitcast_fusion.1
  260.7 1.3 maximum_convert_fusion
  262.0 1.6 copy.78
  263.7 2.3 convert_element_type.184
  266.0 4.7 convolution_convert_fusion.1
  270.8 2.3 reshape.285
  273.2 0.8 add.65
  274.0 0.8 copy.76
  274.7 1.6 multiply_reduce_fusion
  276.4 3.8 fusion.113
  280.3 2.1 fusion.42
  282.5 2.5 reshape.277
  285.1 3.4 multiply_convert_fusion
  288.4 5.8 all-to-all-start.2
  294.3 1.5 convolution_bitcast_fusion.2
  295.7 106.8 %psum.22 = f32[1024,8]{0,1:T(8,128)S(1)} all-reduce(f32[1024,8]{0,1:T(8,128)S(1)} %convolution_bitcast_fusion.2), channel_id=1, replica_groups=mesh['env'=4,'tm'=64] {'env','tm'}, use_global_device_ids=true, to_apply=%region_19.20 | all-reduce | flops 8192 | bytes 65536 | tf_op jit(solution)/shard_map/psum | solution.py:111
  402.7 0.8 fusion.91
  403.5 155.7 %psum.23 = f32[1024]{0:T(1024)S(1)} all-reduce(f32[1024]{0:T(1024)S(1)} %get-tuple-element.21), channel_id=1, replica_groups=mesh['env'=4,'tm'=64] {'tm'}, use_global_device_ids=true, to_apply=%region_21.22 | all-reduce | flops 1024 | bytes 8192 | tf_op jit(solution)/shard_map/psum | solution.py:115
  559.3 0.7 broadcast_multiply_fusion
  560.0 2.0 squeeze.21
  562.0 2.6 convolution_convert_fusion.5
  564.6 2.0 copy.94
  566.7 2.7 fusion.6
  569.4 1.0 convert_reduce_fusion
  570.9 1.2 fusion.25
  572.2 1.2 fusion.24
  573.6 0.7 slice-done.1
  574.3 2.9 fusion.52
  577.2 38.9 %reduce-scatter.2.cloned.1.call-done = bf16[16,2048]{1,0:T(8,128)(2,1)} async-done(((bf16[1024,2048]{1,0:T(8,128)(2,1)}), bf16[16,2048]{1,0:T(8,128)(2,1)}) %reduce-scatter.2.cloned.1.call-update) | async-done | bytes 65552 | tf_op jit(solution)/shard_map/reduce_scatter | solution.py:109
  616.2 2.3 fusion.67
  618.5 82.8 %all-reduce.6.cloned.1.call-done = bf16[16,2048]{1,0:T(8,128)(2,1)} async-done(((bf16[16,2048]{1,0:T(8,128)(2,1)}), bf16[16,2048]{1,0:T(8,128)(2,1)}) %all-reduce.6.cloned.1.call-update) | async-done | bytes 65552 | tf_op jit(solution)/shard_map/psum | solution.py:110
  701.3 0.8 convert_element_type.204
  (107 shorter events, 9.3 us)
Async XLA Ops:
  7.2 184.9 %copy-start = (bf16[1024,1024]{1,0:T(8,128)(2,1)S(1)}, bf16[1024,1024]{1,0:T(8,128)(2,1)}, u32[]{:S(2)}) copy-start(bf16[1024,1024]{1,0:T(8,128)(2,1)} %param.17) | copy-start | bytes 6291460
  7.2 238.1 %all-gather.2.cloned.1.call-start = ((), (), s32[]{:S(2)}) async-start(), calls=%async_computation.4 | async-start | bytes 4259840 | tf_op jit(solution)/shard_map/all_gather | solution.py:98
  172.8 0.6 copy-start.17
  175.1 27.8 %all-to-all-start.1 = ((f32[64,1,128]{2,1,0:T(1,128)}), f32[64,1,128]{2,1,0:T(1,128)S(1)}, u32[]{:S(2)}, u32[]{:S(2)}) async-start(f32[64,1,128]{2,1,0:T(1,128)} %reshape.296), calls=%async_computation.1 | async-start | bytes 65536 | tf_op jit(solution)/shard_map/all_to_all | solution.py:97
  181.6 4.9 copy-start.20
  181.6 4.9 copy-start.25
  187.8 2.1 copy-start.8
  189.2 0.8 copy-start.10
  189.9 1.4 copy-start.1
  190.3 1.4 copy-start.7
  190.3 1.7 copy-start.4
  194.6 21.1 %copy-start.22 = (s32[1,64,4]{1,2,0:T(4,128)S(1)}, s32[1,64,4]{1,2,0:T(4,128)}, u32[]{:S(2)}) copy-start(s32[1,64,4]{1,2,0:T(4,128)} %param.13) | copy-start | bytes 3076
  202.8 30.9 %copy-start.13 = (f32[1024]{0:T(1024)S(1)}, f32[1024]{0:T(1024)}, u32[]{:S(2)}) copy-start(f32[1024]{0:T(1024)} %param.21) | copy-start | bytes 12292
  202.9 26.5 %all-to-all-start = ((bf16[64,2,2048]{2,1,0:T(2,128)(2,1)}), bf16[64,2,2048]{2,1,0:T(2,128)(2,1)}, u32[]{:S(2)}, u32[]{:S(2)}) async-start(bf16[64,2,2048]{2,1,0:T(2,128)(2,1)} %reshape.294), calls=%async_computation | async-start | bytes 1048576 | tf_op jit(solution)/shard_map/all_to_all | solution.py:102
  215.5 400.6 %reduce-scatter.2.cloned.1.call-start = ((), (), s32[]{:S(2)}) async-start(), calls=%async_computation.5 | async-start | bytes 4259840 | tf_op jit(solution)/shard_map/reduce_scatter | solution.py:109
  238.1 7.2 %copy-start.15 = (f32[1024]{0:T(1024)S(1)}, f32[1024]{0:T(1024)}, u32[]{:S(2)}) copy-start(f32[1024]{0:T(1024)} %param.18) | copy-start | bytes 12292
  250.4 3.0 copy-start.23
  250.4 3.0 copy-start.24
  250.4 3.0 copy-start.27
  254.0 6.7 copy-start.19
  276.4 3.9 copy-start.3
  276.4 3.9 copy-start.16
  280.3 4.7 copy-start.14
  285.1 117.7 %copy-start.18 = (f32[1024]{0:T(1024)S(1)}, f32[1024]{0:T(1024)}, u32[]{:S(2)}) copy-start(f32[1024]{0:T(1024)} %copy-done.17) | copy-start | bytes 12292
  288.4 271.6 %all-to-all-start.2 = ((bf16[64,4,1024]{2,1,0:T(4,128)(2,1)}), bf16[64,4,1024]{2,1,0:T(4,128)(2,1)}, u32[]{:S(2)}, u32[]{:S(2)}) async-start(bf16[64,4,1024]{2,1,0:T(4,128)(2,1)} %get-tuple-element.18), calls=%async_computation.2 | async-start | bytes 1048576 | tf_op jit(solution)/shard_map/all_to_all | solution.py:106
  294.2 407.1 %all-reduce.6.cloned.1.call-start = ((), (), s32[]{:S(2)}) async-start(), calls=%async_computation.6 | async-start | bytes 131072 | tf_op jit(solution)/shard_map/psum | solution.py:110
  566.7 2.7 copy-start.2
  569.3 1.0 copy-start.6
  569.4 1.5 copy-start.9
  570.9 1.2 copy-start.11
  570.9 2.4 slice-start
  572.1 1.5 copy-start.5
  572.1 2.2 slice-start.1
  572.1 2.2 copy-start.28
  574.3 2.9 copy-start.21
  574.3 41.8 %copy-start.12 = (bf16[256,1024]{1,0:T(8,128)(2,1)S(1)}, bf16[256,1024]{1,0:T(8,128)(2,1)}, u32[]{:S(2)}) copy-start(bf16[256,1024]{1,0:T(8,128)(2,1)} %squeeze.21) | copy-start | bytes 1572868
  574.3 41.8 %copy-start.26 = (f32[256]{0:T(256)S(1)}, f32[256]{0:T(256)}, u32[]{:S(2)}) copy-start(f32[256]{0:T(256)} %copy-done.25) | copy-start | bytes 3076
Sparse Core Ops, SparseCore 0:
  12.1 128.4 all-gather.1
  270.8 345.2 reduce-scatter.1
  618.9 82.3 all-reduce.5
